TPU v7x, 128 devices: a whole 4x4x4 slice. The times are simulated.
128 devices in a mesh: expert: 8 (over y, z_lo), fsdp: 16 (over x, z_hi, core).
Axes of the slice: x: 4, y: 4, z: 4 (z_hi: 2, z_lo: 2; z = z_hi * 2 + z_lo), core: 2. Of those that a mesh axis runs over, the one named last changes fastest.
Arguments:
- tokens: bfloat16 [18432, 2048], P(('expert', 'fsdp')), may hold values from -6 to 6
- expert_ids: int32 [18432, 6], P(('expert', 'fsdp')), may hold values from 0 to 15, as said below
- combine: float32 [18432, 6], P(('expert', 'fsdp')), may hold values from 0.05 to 1
- gate_weight: bfloat16 [16, 1408, 2048], P('expert', 'fsdp'), may hold values from -0.125 to 0.125
- up_weight: bfloat16 [16, 1408, 2048], P('expert', 'fsdp'), may hold values from -0.125 to 0.125
- down_weight: bfloat16 [16, 1408, 2048], P('expert', 'fsdp'), may hold values from -0.15625 to 0.15625
Outputs:
- mixed: bfloat16 [18432, 2048], P(('expert', 'fsdp'))
Inputs may be any that keep to these rules, and one draw needn't show every extreme that they name: `expert_ids`: each row names 6 different experts. Within the 144 rows of each device no expert is named more than 72 times, and one and the same expert is named exactly 72 times by the rows of every device.
All inputs are finite; a program needn't handle non-finite values.
Results may differ from a plain program's by a relative error of at most 0.0058.
Values may be sent and summed in bfloat16 or wider, within the bound.
A program may use at most 128 MiB of HBM per device.

v0:
```python
import jax
import jax.numpy as jnp
from jax import lax
from jax.sharding import PartitionSpec as P

CAP = 72


def add_piece(expert_rows, pieces):
    gate_piece, up_piece, down_piece = pieces
    gate_pre = jnp.einsum(
        "grd,gfd->grf", expert_rows, gate_piece, preferred_element_type=jnp.float32
    )
    up_pre = jnp.einsum("grd,gfd->grf", expert_rows, up_piece, preferred_element_type=jnp.float32)
    hidden = (jax.nn.silu(gate_pre) * up_pre).astype(jnp.bfloat16)
    return jnp.einsum("grf,gfd->grd", hidden, down_piece, preferred_element_type=jnp.float32)


def per_device(tokens, expert_ids, combine, gate_weight, up_weight, down_weight):
    groups = lax.axis_size("expert")
    per_group = gate_weight.shape[0]
    tok_rows, top_k = expert_ids.shape
    model_width = tokens.shape[1]
    flat_ids = expert_ids.reshape(-1)
    onehot = (flat_ids[:, None] == jnp.arange(per_group * groups, dtype=jnp.int32)[None, :]).astype(
        jnp.int32
    )
    earlier = jnp.cumsum(onehot, axis=0) - onehot
    rank_within = jnp.sum(earlier * onehot, axis=1)
    owner_group = flat_ids // per_group
    within = flat_ids % per_group
    slot_index = (within * groups + owner_group) * CAP + rank_within
    source = jnp.arange(tok_rows * top_k, dtype=jnp.int32) // top_k
    outgoing = (
        jnp.zeros((per_group * groups * CAP, model_width), jnp.bfloat16)
        .at[slot_index]
        .set(tokens[source])
    )
    outgoing = outgoing.reshape(per_group, groups, CAP, model_width)
    arrived = lax.all_to_all(outgoing, "expert", split_axis=1, concat_axis=1, tiled=True)
    expert_rows = arrived.reshape(per_group, groups * CAP, model_width)
    summed = add_piece(
        expert_rows,
        (
            lax.all_gather(gate_weight, "fsdp", axis=1, tiled=True),
            lax.all_gather(up_weight, "fsdp", axis=1, tiled=True),
            lax.all_gather(down_weight, "fsdp", axis=1, tiled=True),
        ),
    )
    produced = summed.astype(jnp.bfloat16)
    produced = produced.reshape(per_group, groups, CAP, model_width)
    returned = lax.all_to_all(produced, "expert", split_axis=1, concat_axis=1, tiled=True)
    back_rows = returned.reshape(per_group * groups * CAP, model_width)[slot_index]
    weighted = (
        back_rows.astype(jnp.float32).reshape(tok_rows, top_k, model_width) * combine[:, :, None]
    )
    return jnp.sum(weighted, axis=1).astype(jnp.bfloat16)


def solution(mesh):
    return jax.shard_map(
        per_device,
        mesh=mesh,
        in_specs=(
            P(("expert", "fsdp"), None),
            P(("expert", "fsdp"), None),
            P(("expert", "fsdp"), None),
            P("expert", "fsdp", None),
            P("expert", "fsdp", None),
            P("expert", "fsdp", None),
        ),
        out_specs=P(("expert", "fsdp"), None),
        check_vma=False,
    )
```

profile of v0, /device:TPU:1, one launch (start us, length us, event | category | flops | bytes accessed | tf_op | source)
XLA Modules:
  0.0 457.1 jit_solution(14942654767058175792)
XLA Ops:
  6.5 0.7 all-gather.4.cloned.1.call-update
  7.3 0.7 all-gather.6.cloned.1.call-update
  8.1 0.7 all-gather.8.cloned.1.call-update
  8.7 0.8 copy.21
  9.5 0.1 eq.24
  9.7 0.1 reshape.195
  9.9 2.0 reduce-window.6
  11.9 0.3 slice_reduce_fusion
  12.4 23.2 %scatter_custom_fusion = bf16[1152,2048]{1,0:T(8,128)(2,1)} fusion(s32[864]{0:T(1024)S(1)} %fusion.5, bf16[144,2048]{1,0:T(8,128)(2,1)S(1)} %copy-done, s32[1024]{0:T(1024)S(1)} %pad_clamp_fusion.1, bf16[]{:T(256)} %constant.42.clone.1), kind=kCustom, calls=%fused_computation.6 | custom fusion | bytes 4718594 | tf_op jit(solution)/shard_map/scatter | solution.py:37
  35.6 2.8 copy.25
  38.4 66.5 %all_to_all.10 = bf16[2,8,72,2048]{3,2,0,1:T(8,128)(2,1)S(1)} all-to-all(bf16[2,8,72,2048]{3,2,0,1:T(8,128)(2,1)S(1)} %copy.25), channel_id=1, replica_groups=mesh['expert'=8,'fsdp'=16] {'expert'}, dimensions={1} | all-to-all | bytes 9437184 | tf_op jit(solution)/shard_map/all_to_all | solution.py:40
  104.9 2.5 copy.26
  107.4 38.9 %all-gather.4.cloned.1.call-done = bf16[2,1408,2048]{2,1,0:T(8,128)(2,1)} async-done(((bf16[2,88,2048]{2,1,0:T(8,128)(2,1)}), bf16[2,1408,2048]{2,1,0:T(8,128)(2,1)}) %all-gather.4.cloned.1.call-update) | async-done | bytes 11534352 | tf_op jit(solution)/shard_map/all_gather | solution.py:45
  146.3 14.4 %fusion.9 = f32[2,576,1408]{2,1,0:T(8,128)} fusion(bf16[2,576,2048]{2,1,0:T(8,128)(2,1)} %bitcast.33, bf16[2,1408,2048]{2,1,0:T(8,128)(2,1)} %all-gather.4.cloned.1.call-done), kind=kOutput, calls=%fused_computation.36 | convolution fusion | flops 6643777536 | bytes 22740992 | tf_op jit(solution)/shard_map/grd,gfd->grf/dot_general | solution.py:11
  160.7 71.9 %all-gather.6.cloned.1.call-done = bf16[2,1408,2048]{2,1,0:T(8,128)(2,1)} async-done(((bf16[2,88,2048]{2,1,0:T(8,128)(2,1)}), bf16[2,1408,2048]{2,1,0:T(8,128)(2,1)}) %all-gather.6.cloned.1.call-update) | async-done | bytes 11534352 | tf_op jit(solution)/shard_map/all_gather | solution.py:46
  232.6 86.3 %all-gather.8.cloned.1.call-done = bf16[2,1408,2048]{2,1,0:T(8,128)(2,1)} async-done(((bf16[2,88,2048]{2,1,0:T(8,128)(2,1)}), bf16[2,1408,2048]{2,1,0:T(8,128)(2,1)}) %all-gather.8.cloned.1.call-update) | async-done | bytes 11534352 | tf_op jit(solution)/shard_map/all_gather | solution.py:47
  318.8 22.8 %convolution_convert_fusion = bf16[2,576,2048]{2,1,0:T(8,128)(2,1)} fusion(bf16[2,1408,2048]{2,1,0:T(8,128)(2,1)} %all-gather.8.cloned.1.call-done, f32[2,576,1408]{2,1,0:T(8,128)} %fusion.9, bf16[2,576,2048]{2,1,0:T(8,128)(2,1)} %bitcast.34, bf16[2,1408,2048]{2,1,0:T(8,128)(2,1)} %all-gather.6.cloned.1.call-done), kind=kOutput, calls=%fused_computation.5 | convolution fusion | flops 13299646464 | bytes 38993920 | tf_op jit(solution)/shard_map/grf,gfd->grd/dot_general | solution.py:16
  341.6 5.2 %copy.27 = bf16[2,8,72,2048]{3,2,0,1:T(8,128)(2,1)} copy(bf16[2,8,72,2048]{3,2,1,0:T(8,128)(2,1)} %bitcast.35) | data formatting | bytes 9437184 | tf_op jit(solution)/shard_map/reshape | solution.py:51
  346.9 4.9 %all-to-all-start.1 = ((bf16[2,8,72,2048]{3,2,0,1:T(8,128)(2,1)}), bf16[2,8,72,2048]{3,2,0,1:T(8,128)(2,1)}, u32[]{:S(2)}, u32[]{:S(2)}) async-start(bf16[2,8,72,2048]{3,2,0,1:T(8,128)(2,1)} %copy.27), calls=%async_computation.1 | async-start | bytes 9437184 | tf_op jit(solution)/shard_map/all_to_all | solution.py:52
  351.9 66.3 %all-to-all-done.1 = bf16[2,8,72,2048]{3,2,0,1:T(8,128)(2,1)} async-done(((bf16[2,8,72,2048]{3,2,0,1:T(8,128)(2,1)}), bf16[2,8,72,2048]{3,2,0,1:T(8,128)(2,1)}, u32[]{:S(2)}, u32[]{:S(2)}) %all-to-all-start.1) | async-done | bytes 4718624 | tf_op jit(solution)/shard_map/all_to_all | solution.py:52
  418.2 5.2 %copy.28 = bf16[2,8,72,2048]{3,2,1,0:T(8,128)(2,1)} copy(bf16[2,8,72,2048]{3,2,0,1:T(8,128)(2,1)} %all-to-all-done.1) | data formatting | bytes 9437184 | tf_op jit(solution)/shard_map/all_to_all | solution.py:52
  423.5 11.7 %gather_fusion = bf16[864,2048]{1,0:T(8,128)(2,1)} fusion(bf16[1152,2048]{1,0:T(8,128)(2,1)} %bitcast.31, s32[1024]{0:T(1024)S(1)} %pad_clamp_fusion), kind=kCustom, calls=%fused_computation.1 | custom fusion | bytes 7081344 | tf_op jit(solution)/shard_map/gather | solution.py:53
  435.2 7.2 %reshape.203 = f32[144,6,2048]{2,1,0:T(8,128)} reshape(bf16[864,2048]{1,0:T(8,128)(2,1)} %gather_fusion) | data formatting | bytes 10616832 | tf_op jit(solution)/shard_map/convert_element_type | solution.py:55
  442.4 8.2 %multiply_reduce_fusion = bf16[144,2048]{1,0:T(8,128)(2,1)} fusion(f32[144,6,2048]{2,1,0:T(8,128)} %reshape.203, f32[144,6]{1,0:T(8,128)S(1)} %copy.29), kind=kLoop, calls=%fused_computation.3 | loop fusion | flops 3244032 | bytes 7671168 | tf_op jit(solution)/shard_map/reduce_sum | solution.py:57
  (19 shorter events, 0.4 us)
Async XLA Ops:
  6.5 5.9 %copy-start = (bf16[144,2048]{1,0:T(8,128)(2,1)S(1)}, bf16[144,2048]{1,0:T(8,128)(2,1)}, u32[]{:S(2)}) copy-start(bf16[144,2048]{1,0:T(8,128)(2,1)} %param.6) | copy-start | bytes 1769476
  6.5 139.8 %all-gather.4.cloned.1.call-start = ((), (), s32[]{:S(2)}) async-start(), calls=%async_computation.2 | async-start | bytes 12255232 | tf_op jit(solution)/shard_map/all_gather | solution.py:45
  7.3 225.3 %all-gather.6.cloned.1.call-start = ((), (), s32[]{:S(2)}) async-start(), calls=%async_computation.3 | async-start | bytes 12255232 | tf_op jit(solution)/shard_map/all_gather | solution.py:46
  8.0 310.8 %all-gather.8.cloned.1.call-start = ((), (), s32[]{:S(2)}) async-start(), calls=%async_computation.4 | async-start | bytes 12255232 | tf_op jit(solution)/shard_map/all_gather | solution.py:47
  346.9 5.0 %copy-start.2 = (f32[144,6]{0,1:T(8,128)S(1)}, f32[144,6]{0,1:T(8,128)}, u32[]{:S(2)}) copy-start(f32[144,6]{0,1:T(8,128)} %param.8) | copy-start | bytes 10372
  346.9 71.4 %all-to-all-start.1 = ((bf16[2,8,72,2048]{3,2,0,1:T(8,128)(2,1)}), bf16[2,8,72,2048]{3,2,0,1:T(8,128)(2,1)}, u32[]{:S(2)}, u32[]{:S(2)}) async-start(bf16[2,8,72,2048]{3,2,0,1:T(8,128)(2,1)} %copy.27), calls=%async_computation.1 | async-start | bytes 9437184 | tf_op jit(solution)/shard_map/all_to_all | solution.py:52
  435.2 15.4 %copy-start.1 = (bf16[144,2048]{1,0:T(8,128)(2,1)S(1)}, bf16[144,2048]{1,0:T(8,128)(2,1)}, u32[]{:S(2)}) copy-start(bf16[144,2048]{1,0:T(8,128)(2,1)} %param.6) | copy-start | bytes 1769476
Sparse Core Ops, SparseCore 0:
  9.8 136.4 all-gather.3
  148.8 83.7 all-gather.5
  235.1 83.7 all-gather.7
where the time goes:
time: 458 us; the launch traced here: 457 us
  waiting for transfers between devices  265 us (58%)
  blocking collectives  66.5 us (15%)
  local copies, waits for them, and re-layouts  59.3 us (13%)
  matrix products  37.2 us (8%)
  between operations  13.2 us (3%)
  other arithmetic  10.4 us (2%)
  starting transfers between devices  5.02 us (1%)
    all_gather x1, waiting for transfers between devices, per_device(): lax.all_gather(down_weight, 'fsdp', axis=1, tiled=True)  86.3 us
    all_gather x1, waiting for transfers between devices, per_device(): lax.all_gather(up_weight, 'fsdp', axis=1, tiled=True)  71.9 us
    all_to_all x1, blocking collectives, per_device(): lax.all_to_all(outgoing, 'expert', split_axis=1, concat_axis=1, tiled=True)  66.5 us
    all_to_all x1, waiting for transfers between devices, per_device(): lax.all_to_all(produced, 'expert', split_axis=1, concat_axis=1, tiled=True)  66.3 us
    all_gather x1, waiting for transfers between devices, per_device(): lax.all_gather(gate_weight, 'fsdp', axis=1, tiled=True)  38.9 us
    scatter x1, local copies, waits for them, and re-layouts, per_device(): outgoing = jnp.zeros((per_group * groups * CAP, model_width), jnp.bfloat1...  23.2 us
    dot_general x1, matrix products, add_piece(): jnp.einsum('grf,gfd->grd', hidden, down_piece, preferred_element_type=jnp...  22.8 us
    dot_general x1, matrix products, add_piece(): jnp.einsum('grd,gfd->grf', expert_rows, gate_piece, preferred_element_typ...  14.4 us
  transfers between devices with their start and end apart: 4, of which 4 were waited for; matrix products, arithmetic and copies ran while one was open for 10% of the time, Pallas kernels for 0%

commit v1 on v0

--- a/solution.py
+++ b/solution.py
@@ -44,7 +44,10 @@
         (
             lax.all_gather(gate_weight, "fsdp", axis=1, tiled=True),
             lax.all_gather(up_weight, "fsdp", axis=1, tiled=True),
-            lax.all_gather(down_weight, "fsdp", axis=1, tiled=True),
+            jnp.concatenate(
+                lax.all_to_all(jnp.stack([down_weight] * lax.axis_size("fsdp")), "fsdp", 0, 0),
+                axis=1,
+            ),
         ),
     )
     produced = summed.astype(jnp.bfloat16)

time: 458 us -> 505 us (1.10)
  the two profiles are of different devices: /device:TPU:1 before, /device:TPU:66 now
where the time goes in v1:
time: 505 us; the launch traced here: 504 us
  waiting for transfers between devices  283 us (56%)
  local copies, waits for them, and re-layouts  77.6 us (15%)
  blocking collectives  69.8 us (14%)
  matrix products  37.1 us (7%)
  between operations  13.5 us (3%)
  starting transfers between devices  12.2 us (2%)
  other arithmetic  10.4 us (2%)
    all_to_all x1, waiting for transfers between devices, per_device(): lax.all_to_all(jnp.stack([down_weight] * lax.axis_size('fsdp')), 'fsdp',...  150 us
    all_to_all x1, blocking collectives, per_device(): lax.all_to_all(outgoing, 'expert', split_axis=1, concat_axis=1, tiled=True)  69.8 us
    all_to_all x1, waiting for transfers between devices, per_device(): lax.all_to_all(produced, 'expert', split_axis=1, concat_axis=1, tiled=True)  67.1 us
    all_gather x1, waiting for transfers between devices, per_device(): lax.all_gather(up_weight, 'fsdp', axis=1, tiled=True)  64.8 us
    scatter x1, local copies, waits for them, and re-layouts, per_device(): outgoing = jnp.zeros((per_group * groups * CAP, model_width), jnp.bfloat1...  23.2 us
    dot_general x1, matrix products, add_piece(): jnp.einsum('grf,gfd->grd', hidden, down_piece, preferred_element_type=jnp...  22.8 us
    dot_general x1, matrix products, add_piece(): jnp.einsum('grd,gfd->grf', expert_rows, gate_piece, preferred_element_typ...  14.4 us
    gather x1, local copies, waits for them, and re-layouts, per_device(): returned.reshape(per_group * groups * CAP, model_width)[slot_index]  11.7 us
  transfers between devices with their start and end apart: 4, of which 3 were waited for; matrix products, arithmetic and copies ran while one was open for 13% of the time, Pallas kernels for 0%

profile of v1, /device:TPU:66, one launch (start us, length us, event | category | flops | bytes accessed | tf_op | source)
XLA Modules:
  0.0 503.7 jit_solution(2212052876440020318)
XLA Ops:
  6.5 0.7 all-gather.3.cloned.1.call-update
  7.3 0.7 all-gather.5.cloned.1.call-update
  8.0 0.8 copy.22
  9.0 0.1 reshape.203
  9.1 2.0 reduce-window.6
  11.1 0.3 slice_reduce_fusion
  11.7 23.2 %scatter_custom_fusion = bf16[1152,2048]{1,0:T(8,128)(2,1)} fusion(s32[864]{0:T(1024)S(1)} %fusion.5, bf16[144,2048]{1,0:T(8,128)(2,1)S(1)} %copy-done, s32[1024]{0:T(1024)S(1)} %pad_clamp_fusion.1, bf16[]{:T(256)} %constant.42.clone.1), kind=kCustom, calls=%fused_computation.6 | custom fusion | bytes 4718594 | tf_op jit(solution)/shard_map/scatter | solution.py:37
  34.9 2.7 copy.26
  37.6 69.8 %all_to_all.15 = bf16[2,8,72,2048]{3,2,0,1:T(8,128)(2,1)} all-to-all(bf16[2,8,72,2048]{3,2,0,1:T(8,128)(2,1)S(1)} %copy.26), channel_id=1, replica_groups=mesh['expert'=8,'fsdp'=16] {'expert'}, dimensions={1} | all-to-all | bytes 9437184 | tf_op jit(solution)/shard_map/all_to_all | solution.py:40
  107.4 5.7 %stack.2 = bf16[16,2,88,2048]{3,2,1,0:T(8,128)(2,1)} broadcast(bf16[2,88,2048]{2,1,0:T(8,128)(2,1)S(1)} %copy-done.2), dimensions={1,2,3} | broadcast | bytes 12255232 | tf_op jit(solution)/shard_map/stack | solution.py:48
  113.1 7.3 %all-to-all-start.1 = ((bf16[16,2,88,2048]{3,2,1,0:T(8,128)(2,1)}), bf16[16,2,88,2048]{3,2,1,0:T(8,128)(2,1)}, u32[]{:S(2)}, u32[]{:S(2)}) async-start(bf16[16,2,88,2048]{3,2,1,0:T(8,128)(2,1)} %stack.2), calls=%async_computation.1 | async-start | bytes 23068672 | tf_op jit(solution)/shard_map/all_to_all | solution.py:48
  120.3 5.2 %copy.27 = bf16[2,8,72,2048]{3,2,1,0:T(8,128)(2,1)} copy(bf16[2,8,72,2048]{3,2,0,1:T(8,128)(2,1)} %all_to_all.15) | data formatting | bytes 9437184 | tf_op jit(solution)/shard_map/all_to_all | solution.py:40
  125.5 149.7 %all-to-all-done.1 = bf16[16,2,88,2048]{3,2,1,0:T(8,128)(2,1)} async-done(((bf16[16,2,88,2048]{3,2,1,0:T(8,128)(2,1)}), bf16[16,2,88,2048]{3,2,1,0:T(8,128)(2,1)}, u32[]{:S(2)}, u32[]{:S(2)}) %all-to-all-start.1) | async-done | bytes 11534368 | tf_op jit(solution)/shard_map/all_to_all | solution.py:48
  275.2 9.9 %copy.28 = bf16[2,16,88,2048]{3,2,1,0:T(8,128)(2,1)} copy(bf16[2,16,88,2048]{3,2,0,1:T(8,128)(2,1)} %bitcast.3) | data formatting | bytes 23068672 | tf_op jit(solution)/shard_map/reshape | solution.py:47
  285.2 14.4 %fusion.9 = f32[2,576,1408]{2,1,0:T(8,128)} fusion(bf16[2,576,2048]{2,1,0:T(8,128)(2,1)} %bitcast.36, bf16[2,1408,2048]{2,1,0:T(8,128)(2,1)} %all-gather.3.cloned.1.call-done), kind=kOutput, calls=%fused_computation.36 | convolution fusion | flops 6643777536 | bytes 22740992 | tf_op jit(solution)/shard_map/grd,gfd->grf/dot_general | solution.py:11
  299.6 64.8 %all-gather.5.cloned.1.call-done = bf16[2,1408,2048]{2,1,0:T(8,128)(2,1)} async-done(((bf16[2,88,2048]{2,1,0:T(8,128)(2,1)}), bf16[2,1408,2048]{2,1,0:T(8,128)(2,1)}) %all-gather.5.cloned.1.call-update) | async-done | bytes 11534352 | tf_op jit(solution)/shard_map/all_gather | solution.py:46
  364.4 22.8 %convolution_convert_fusion = bf16[2,576,2048]{2,1,0:T(8,128)(2,1)} fusion(bf16[2,1408,2048]{2,1,0:T(8,128)(2,1)} %bitcast.35, f32[2,576,1408]{2,1,0:T(8,128)} %fusion.9, bf16[2,576,2048]{2,1,0:T(8,128)(2,1)} %bitcast.37, bf16[2,1408,2048]{2,1,0:T(8,128)(2,1)} %all-gather.5.cloned.1.call-done), kind=kOutput, calls=%fused_computation.5 | convolution fusion | flops 13299646464 | bytes 38993920 | tf_op jit(solution)/shard_map/grf,gfd->grd/dot_general | solution.py:16
  387.1 5.2 %copy.29 = bf16[2,8,72,2048]{3,2,0,1:T(8,128)(2,1)} copy(bf16[2,8,72,2048]{3,2,1,0:T(8,128)(2,1)} %bitcast.38) | data formatting | bytes 9437184 | tf_op jit(solution)/shard_map/reshape | solution.py:54
  392.4 4.9 all-to-all-start.2
  397.4 67.1 %all-to-all-done.2 = bf16[2,8,72,2048]{3,2,0,1:T(8,128)(2,1)} async-done(((bf16[2,8,72,2048]{3,2,0,1:T(8,128)(2,1)}), bf16[2,8,72,2048]{3,2,0,1:T(8,128)(2,1)}, u32[]{:S(2)}, u32[]{:S(2)}) %all-to-all-start.2) | async-done | bytes 4718624 | tf_op jit(solution)/shard_map/all_to_all | solution.py:55
  464.6 5.2 %copy.30 = bf16[2,8,72,2048]{3,2,1,0:T(8,128)(2,1)} copy(bf16[2,8,72,2048]{3,2,0,1:T(8,128)(2,1)} %all-to-all-done.2) | data formatting | bytes 9437184 | tf_op jit(solution)/shard_map/all_to_all | solution.py:55
  469.8 11.7 %gather_fusion = bf16[864,2048]{1,0:T(8,128)(2,1)} fusion(bf16[1152,2048]{1,0:T(8,128)(2,1)} %bitcast.33, s32[1024]{0:T(1024)S(1)} %pad_clamp_fusion), kind=kCustom, calls=%fused_computation.1 | custom fusion | bytes 7081344 | tf_op jit(solution)/shard_map/gather | solution.py:56
  481.5 7.2 %reshape.213 = f32[144,6,2048]{2,1,0:T(8,128)} reshape(bf16[864,2048]{1,0:T(8,128)(2,1)} %gather_fusion) | data formatting | bytes 10616832 | tf_op jit(solution)/shard_map/convert_element_type | solution.py:58
  488.7 8.2 %multiply_reduce_fusion = bf16[144,2048]{1,0:T(8,128)(2,1)} fusion(f32[144,6,2048]{2,1,0:T(8,128)} %reshape.213, f32[144,6]{1,0:T(8,128)S(1)} %copy.31), kind=kLoop, calls=%fused_computation.3 | loop fusion | flops 3244032 | bytes 7671168 | tf_op jit(solution)/shard_map/reduce_sum | solution.py:60
  (22 shorter events, 0.5 us)
Async XLA Ops:
  6.5 5.1 %copy-start = (bf16[144,2048]{1,0:T(8,128)(2,1)S(1)}, bf16[144,2048]{1,0:T(8,128)(2,1)}, u32[]{:S(2)}) copy-start(bf16[144,2048]{1,0:T(8,128)(2,1)} %param.6) | copy-start | bytes 1769476
  6.5 278.6 %all-gather.3.cloned.1.call-start = ((), (), s32[]{:S(2)}) async-start(), calls=%async_computation.3 | async-start | bytes 12255232 | tf_op jit(solution)/shard_map/all_gather | solution.py:45
  7.3 357.1 %all-gather.5.cloned.1.call-start = ((), (), s32[]{:S(2)}) async-start(), calls=%async_computation.4 | async-start | bytes 12255232 | tf_op jit(solution)/shard_map/all_gather | solution.py:46
  37.6 69.8 %copy-start.2 = (bf16[2,88,2048]{2,1,0:T(8,128)(2,1)S(1)}, bf16[2,88,2048]{2,1,0:T(8,128)(2,1)}, u32[]{:S(2)}) copy-start(bf16[2,88,2048]{2,1,0:T(8,128)(2,1)} %param.11) | copy-start | bytes 2162692
  113.1 162.2 %all-to-all-start.1 = ((bf16[16,2,88,2048]{3,2,1,0:T(8,128)(2,1)}), bf16[16,2,88,2048]{3,2,1,0:T(8,128)(2,1)}, u32[]{:S(2)}, u32[]{:S(2)}) async-start(bf16[16,2,88,2048]{3,2,1,0:T(8,128)(2,1)} %stack.2), calls=%async_computation.1 | async-start | bytes 23068672 | tf_op jit(solution)/shard_map/all_to_all | solution.py:48
  392.4 5.0 copy-start.3
  392.4 72.2 %all-to-all-start.2 = ((bf16[2,8,72,2048]{3,2,0,1:T(8,128)(2,1)}), bf16[2,8,72,2048]{3,2,0,1:T(8,128)(2,1)}, u32[]{:S(2)}, u32[]{:S(2)}) async-start(bf16[2,8,72,2048]{3,2,0,1:T(8,128)(2,1)} %copy.29), calls=%async_computation.2 | async-start | bytes 9437184 | tf_op jit(solution)/shard_map/all_to_all | solution.py:55
  481.5 15.4 %copy-start.1 = (bf16[144,2048]{1,0:T(8,128)(2,1)S(1)}, bf16[144,2048]{1,0:T(8,128)(2,1)}, u32[]{:S(2)}) copy-start(bf16[144,2048]{1,0:T(8,128)(2,1)} %param.6) | copy-start | bytes 1769476
Sparse Core Ops, SparseCore 0:
  9.8 169.4 all-gather.2
  181.8 182.5 all-gather.4
